TPU v7x, 32 devices: a whole 2x2x4 slice. The times are simulated.
32 devices in a mesh: groups: 2 (over y), seq: 4 (over z), head: 4 (over x, core).
Axes of the slice: x: 2, y: 2, z: 4, core: 2. Of those that a mesh axis runs over, the one named last changes fastest.
Arguments:
- doc_start: int32 [1024], P(('groups', 'seq')), parts along dimension 0, may hold values from 0 to 511, as said below
- q_gdn: bfloat16 [1024, 2048], P(('groups', 'seq'), 'head'), parts along dimension 0, may hold values from -6 to 6
- k_gdn: bfloat16 [1024, 2048], P(('groups', 'seq'), 'head'), parts along dimension 0, may hold values from -6 to 6
- v_gdn: bfloat16 [1024, 4096], P(('groups', 'seq'), 'head'), parts along dimension 0, may hold values from -6 to 6
- z_gdn: bfloat16 [1024, 4096], P(('groups', 'seq'), 'head'), parts along dimension 0, may hold values from -6 to 6
- beta_logit: float32 [32, 1024], P('head', ('groups', 'seq')), parts along dimension 1, may hold values from -8 to 3
- log_decay: float32 [32, 1024], P('head', ('groups', 'seq')), parts along dimension 1, may hold values from -1 to 0
- norm_weight: float32 [128], replicated, may hold values from 0.1 to 1.9
- q_attn: bfloat16 [1024, 4096], P(('groups', 'seq'), 'head'), parts along dimension 0, may hold values from -6 to 6
- k_attn: bfloat16 [1024, 512], P(('groups', 'seq')), parts along dimension 0, may hold values from -6 to 6
- v_attn: bfloat16 [1024, 512], P(('groups', 'seq')), parts along dimension 0, may hold values from -6 to 6
- gate_attn: bfloat16 [1024, 4096], P(('groups', 'seq'), 'head'), parts along dimension 0, may hold values from -6 to 6
Outputs:
- gdn_out: bfloat16 [1024, 4096], P(('groups', 'seq'), 'head'), parts along dimension 0
- attn_out: bfloat16 [1024, 4096], P(('groups', 'seq'), 'head'), parts along dimension 0
There are 2 independent parts, one for each index of `groups`. A program takes and returns all parts, laid end to end along the dimension named above; an argument that names none is the same for every part. Nothing has to cross between parts.
Inputs may be any that keep to these rules, and one draw needn't show every extreme that they name: Nondecreasing; doc_start[i] <= i, with equality exactly at the first token of each of the 3 documents; the first document starts at 0.
All inputs are finite; a program needn't handle non-finite values.
Results may differ from a plain program's by a relative error of at most 0.0095.
Values may be sent and summed in bfloat16 or wider, within the bound.
A program may use at most 128 MiB of HBM per device.

v0:
```python
import jax
import jax.numpy as jnp
from jax import lax
from jax.sharding import PartitionSpec as P

DK = 128
DV = 128
QH = 16
KVH = 2
HD_A = 256
BLOCK = 64
HIGH = lax.Precision.HIGHEST


def shifted(shard, axis, by):
    length = lax.axis_size(axis)
    pairs = [(i, i + by) for i in range(length) if 0 <= i + by < length]
    return lax.ppermute(shard, axis, pairs)


def unit_rows(values):
    return values * lax.rsqrt(jnp.sum(values * values, axis=-1, keepdims=True) + 1e-06)


def blocked(values, count):
    length, heads, width = values.shape
    return values.reshape(count, length // count, heads, width).transpose(0, 2, 1, 3)


def block_terms(anchor, doc_block, query, keys, values, beta, log_gate):
    width = query.shape[1]
    running = jnp.cumsum(log_gate, axis=1)
    place = anchor + jnp.arange(width, dtype=jnp.int32)
    causal = place[None, :] <= place[:, None]
    same = causal & (doc_block[:, None] <= place[None, :])
    strict = same & (place[None, :] < place[:, None])
    spread = jnp.where(same[None], running[:, :, None] - running[:, None, :], 0.0)
    decay = jnp.where(same[None], jnp.exp(spread), 0.0)
    alive = (doc_block < anchor).astype(jnp.float32)
    entry = jnp.exp(running) * alive[None, :]
    gram = jnp.einsum("hik,hjk->hij", keys, keys, precision=HIGH)
    lower_part = jnp.where(strict[None], decay * gram, 0.0)
    system = jnp.eye(width, dtype=jnp.float32)[None] + beta[:, :, None] * lower_part
    right = jnp.concatenate([beta[:, :, None] * values, (beta * entry)[:, :, None] * keys], axis=2)
    solved = lax.linalg.triangular_solve(
        system, right, left_side=True, lower=True, unit_diagonal=True
    )
    fresh = solved[:, :, : values.shape[2]]
    erased = solved[:, :, values.shape[2] :]
    scores = jnp.einsum("hik,hjk->hij", query, keys, precision=HIGH) * decay
    local_out = jnp.einsum("hij,hjv->hiv", scores, fresh, precision=HIGH)
    reach = entry[:, :, None] * query - jnp.einsum("hij,hjk->hik", scores, erased, precision=HIGH)
    tail_keys = decay[:, -1, :, None] * keys
    identity = jnp.eye(keys.shape[2], dtype=jnp.float32)
    carry_map = entry[:, -1, None, None] * identity[None] - jnp.einsum(
        "hjk,hjl->hkl", erased, tail_keys, precision=HIGH
    )
    carry_add = jnp.einsum("hjv,hjk->hvk", fresh, tail_keys, precision=HIGH)
    return (local_out, reach, carry_map, carry_add)


def compose(earlier, later):
    joined_map = jnp.einsum("hkl,hlm->hkm", earlier[0], later[0], precision=HIGH)
    joined_add = jnp.einsum("hvl,hlm->hvm", earlier[1], later[0], precision=HIGH) + later[1]
    return (joined_map, joined_add)


def entering_state(device_map, device_add):

    def relay(turn, pair):
        incoming, state = pair
        incoming = shifted(state.astype(jnp.bfloat16), "seq", 1).astype(state.dtype)
        state = jnp.einsum("hvk,hkl->hvl", incoming, device_map, precision=HIGH) + device_add
        return (incoming, state)

    start_state, _ = lax.fori_loop(
        0, lax.axis_size("seq") - 1, relay, (jnp.zeros_like(device_add), device_add)
    )
    return start_state


def delta_layer(doc_start, q_gdn, k_gdn, v_gdn, z_gdn, beta_logit, log_decay, norm_weight, anchor):
    length = q_gdn.shape[0]
    key_heads = q_gdn.shape[1] // DK
    value_heads = v_gdn.shape[1] // DV
    repeat = value_heads // key_heads
    count = length // BLOCK
    query = jnp.repeat(
        unit_rows(q_gdn.astype(jnp.float32).reshape(length, key_heads, DK)), repeat, axis=1
    )
    keys = jnp.repeat(
        unit_rows(k_gdn.astype(jnp.float32).reshape(length, key_heads, DK)), repeat, axis=1
    )
    values = v_gdn.astype(jnp.float32).reshape(length, value_heads, DV)
    beta = jax.nn.sigmoid(beta_logit).reshape(value_heads, count, BLOCK).transpose(1, 0, 2)
    log_gate = log_decay.reshape(value_heads, count, BLOCK).transpose(1, 0, 2)
    docs = doc_start.reshape(count, BLOCK)
    anchors = anchor + BLOCK * jnp.arange(count, dtype=jnp.int32)
    identity = jnp.broadcast_to(jnp.eye(DK, dtype=jnp.float32), (value_heads, DK, DK))

    def sweep(totals, inputs):
        total_map, total_add = totals
        block_anchor, doc_block, q_block, k_block, v_block, b_block, g_block = inputs
        local_out, reach, carry_map, carry_add = block_terms(
            block_anchor, doc_block, q_block, k_block, v_block, b_block, g_block
        )
        joined = compose((total_map, total_add), (carry_map, carry_add))
        return (joined, (local_out, reach, total_map, total_add))

    start_totals = (identity, jnp.zeros((value_heads, DV, DK), jnp.float32))
    scanned = (
        anchors,
        docs,
        blocked(query, count),
        blocked(keys, count),
        blocked(values, count),
        beta,
        log_gate,
    )
    (device_map, device_add), (local_out, reach, prefix_map, prefix_add) = lax.scan(
        sweep, start_totals, scanned
    )
    start_state = entering_state(device_map, device_add)
    block_state = jnp.einsum("hvk,chkl->chvl", start_state, prefix_map, precision=HIGH) + prefix_add
    mixed = local_out + jnp.einsum("chik,chvk->chiv", reach, block_state, precision=HIGH)
    mixed = mixed.transpose(0, 2, 1, 3).reshape(length, value_heads, DV)
    gate = z_gdn.astype(jnp.float32).reshape(length, value_heads, DV)
    factor = lax.rsqrt(jnp.mean(mixed * mixed, axis=-1, keepdims=True) + 1e-06)
    normed = mixed * factor * norm_weight * jax.nn.silu(gate)
    return normed.reshape(length, value_heads * DV).astype(jnp.bfloat16)


def attend(doc_start, q_attn, k_attn, v_attn, gate_attn, anchor):
    length = q_attn.shape[0]
    local_heads = q_attn.shape[1] // HD_A
    group = QH // KVH
    shards_seen = lax.axis_size("seq") // 2 + 1
    window_size = shards_seen * length
    kv_head = lax.axis_index("head") * local_heads // group
    keys_own = lax.dynamic_slice_in_dim(k_attn, kv_head * HD_A, HD_A, 1)
    values_own = lax.dynamic_slice_in_dim(v_attn, kv_head * HD_A, HD_A, 1)
    query = q_attn.reshape(length, local_heads, HD_A)
    q_place = anchor + jnp.arange(length, dtype=jnp.int32)
    lower = jnp.maximum(doc_start, q_place - window_size + 1)
    lowest = jnp.min(lower)
    highest = anchor + length - 1
    factor = HD_A ** (-0.5)
    initial = (
        jnp.full((local_heads, length), -1e30, jnp.float32),
        jnp.zeros((local_heads, length), jnp.float32),
        jnp.zeros((local_heads, length, HD_A), jnp.float32),
    )
    key_piece = lax.all_gather(keys_own, "seq", axis=0, tiled=True)
    value_piece = lax.all_gather(values_own, "seq", axis=0, tiled=True)
    count = key_piece.shape[0]
    width = count
    while width > 1024 and width % 2 == 0:
        width = width // 2

    def one(index, inner):
        begin = index * width
        key_part = lax.dynamic_slice_in_dim(key_piece, begin, width, 0)
        value_part = lax.dynamic_slice_in_dim(value_piece, begin, width, 0)
        k_place = begin + jnp.arange(width, dtype=jnp.int32)

        def compute(state):
            peak, total, accum = state
            scores = (
                jnp.einsum("qhd,kd->hqk", query, key_part, preferred_element_type=jnp.float32)
                * factor
            )
            visible = (k_place[None, :] >= lower[:, None]) & (k_place[None, :] <= q_place[:, None])
            masked = jnp.where(visible[None], scores, -jnp.inf)
            new_peak = jnp.maximum(peak, jnp.max(masked, axis=-1))
            weights = jnp.exp(masked - new_peak[:, :, None])
            shrink = jnp.exp(peak - new_peak)
            total = total * shrink + jnp.sum(weights, axis=-1)
            update = jnp.einsum(
                "hqk,kd->hqd",
                weights.astype(jnp.bfloat16),
                value_part,
                preferred_element_type=jnp.float32,
            )
            accum = accum * shrink[:, :, None] + update
            return (new_peak, total, accum)

        def unchanged(state):
            return state

        busy = (begin <= highest) & (begin + width - 1 >= lowest)
        return lax.cond(busy, compute, unchanged, inner)

    peak, total, accum = lax.fori_loop(0, count // width, one, initial)
    mixed = (accum / total[:, :, None]).transpose(1, 0, 2).reshape(length, local_heads * HD_A)
    return (mixed * jax.nn.sigmoid(gate_attn.astype(jnp.float32))).astype(jnp.bfloat16)


def shards(
    doc_start,
    q_gdn,
    k_gdn,
    v_gdn,
    z_gdn,
    beta_logit,
    log_decay,
    norm_weight,
    q_attn,
    k_attn,
    v_attn,
    gate_attn,
):
    anchor = lax.axis_index("seq") * q_gdn.shape[0]
    gdn_out = delta_layer(
        doc_start, q_gdn, k_gdn, v_gdn, z_gdn, beta_logit, log_decay, norm_weight, anchor
    )
    attn_out = attend(doc_start, q_attn, k_attn, v_attn, gate_attn, anchor)
    return (gdn_out, attn_out)


def solution(mesh):
    return jax.shard_map(
        shards,
        mesh=mesh,
        in_specs=(
            P(("groups", "seq")),
            P(("groups", "seq"), "head"),
            P(("groups", "seq"), "head"),
            P(("groups", "seq"), "head"),
            P(("groups", "seq"), "head"),
            P("head", ("groups", "seq")),
            P("head", ("groups", "seq")),
            P(),
            P(("groups", "seq"), "head"),
            P(("groups", "seq"), None),
            P(("groups", "seq"), None),
            P(("groups", "seq"), "head"),
        ),
        out_specs=(P(("groups", "seq"), "head"), P(("groups", "seq"), "head")),
        check_vma=False,
    )
```

profile of v0, /device:TPU:0, one launch (start us, length us, event | category | flops | bytes accessed | tf_op | source)
XLA Modules:
  0.0 189.3 jit_solution(7092509554987152704)
XLA Ops:
  0.7 1.0 reshape.347
  3.7 0.9 copy-done.13
  7.8 105.6 %while.13 = (s32[]{:T(128)}, f32[8,128,128]{1,2,0:T(8,128)S(1)}, f32[8,128,128]{1,2,0:T(8,128)S(1)}, f32[2,8,64,128]{3,2,1,0:T(8,128)}, f32[2,8,64,128]{3,2,1,0:...) while((s32[]{:T(128)}, f32[8,128,128]{1,2,0:T(8,128)S(1)}, ...), condition=%wide.region_4.5_spmd.clone, body=%wide.region_2.4_spmd.clone.sunk | while | flops 907780864 | bytes 40192524 | solution.py:120
  10.1 39.3 %custom-call.11 = f32[8,1,64,64]{2,3,1,0:T(8,128)S(1)} custom-call(f32[8,1,64,64]{3,2,1,0:T(8,128)S(1)} %fusion.124), custom_call_target="InvertDiagBlocksLowerTriangular" | custom-call | tf_op jit(solution)/shard_map/while/body/eval_jaxpr/triangular_solve | solution.py:45
  50.3 1.0 constant_dynamic-slice_fusion.9
  52.4 1.1 convolution_subtract_fusion.3
  53.5 1.0 convolution_bitcast_fusion.7
  55.2 1.1 convolution_add_fusion.7
  56.3 1.0 convolution_bitcast_fusion.6
  62.9 39.3 %custom-call.11 = f32[8,1,64,64]{2,3,1,0:T(8,128)S(1)} custom-call(f32[8,1,64,64]{3,2,1,0:T(8,128)S(1)} %fusion.124), custom_call_target="InvertDiagBlocksLowerTriangular" | custom-call | tf_op jit(solution)/shard_map/while/body/eval_jaxpr/triangular_solve | solution.py:45
  103.1 1.0 constant_dynamic-slice_fusion.9
  105.2 1.1 convolution_subtract_fusion.3
  106.3 1.0 convolution_bitcast_fusion.7
  108.0 1.1 convolution_add_fusion.7
  109.1 1.0 convolution_bitcast_fusion.6
  114.6 34.6 %while.12 = (s32[]{:T(128)}, f32[8,128,128]{2,1,0:T(8,128)}, bf16[8,128,128]{2,1,0:T(8,128)(2,1)}, f32[8,128,128]{2,1,0:T(8,128)S(1)}, f32[8,128,128]{2,1,0:T(8,128)S(1)}, /*index=5*/s32[]{:T(128)}) while((s32[]{:T(128)}, f32[8,128,128]{2,1,0:T(8,128)}, bf16[8,128,128]{2,1,0:T(8,128)(2,1)}, f32[8,128,128]{2,1,0:T(8,128)S(1)}, ...), condition=%wide.region_6.7_spmd, body=%wide.region_5.6_spmd.sunk | while | flops 201719808 | bytes 3407981 | solution.py:76
  114.6 5.1 %collective-permute-start = (bf16[8,128,128]{2,1,0:T(8,128)(2,1)}, bf16[8,128,128]{2,1,0:T(8,128)(2,1)S(1)}, u32[]{:S(2)}, u32[]{:S(2)}) collective-permute-start(bf16[8,128,128]{2,1,0:T(8,128)(2,1)} %get-tuple-element.581), channel_id=1, source_target_pairs={{0,4},{4,8},{8,12},{1,5},{5,9},{9,13},{2,6},{6,10},{10,14},{3,7},{... | collective-permute-start | bytes 786440 | tf_op jit(solution)/shard_map/while/body/eval_jaxpr/ppermute | solution.py:18
  119.8 5.8 %collective-permute-done = bf16[8,128,128]{2,1,0:T(8,128)(2,1)S(1)} collective-permute-done((bf16[8,128,128]{2,1,0:T(8,128)(2,1)}, bf16[8,128,128]{2,1,0:T(8,128)(2,1)S(1)}, u32[]{:S(2)}, u32[]{:S(2)}) %collective-permute-start) | collective-permute-done | bytes 262176 | tf_op jit(solution)/shard_map/while/body/eval_jaxpr/ppermute | solution.py:18
  126.4 1.1 convolution_add_fusion.6
  127.5 4.3 %collective-permute-start = (bf16[8,128,128]{2,1,0:T(8,128)(2,1)}, bf16[8,128,128]{2,1,0:T(8,128)(2,1)S(1)}, u32[]{:S(2)}, u32[]{:S(2)}) collective-permute-start(bf16[8,128,128]{2,1,0:T(8,128)(2,1)} %get-tuple-element.581), channel_id=1, source_target_pairs={{0,4},{4,8},{8,12},{1,5},{5,9},{9,13},{2,6},{6,10},{10,14},{3,7},{... | collective-permute-start | bytes 786440 | tf_op jit(solution)/shard_map/while/body/eval_jaxpr/ppermute | solution.py:18
  131.8 5.0 %collective-permute-done = bf16[8,128,128]{2,1,0:T(8,128)(2,1)S(1)} collective-permute-done((bf16[8,128,128]{2,1,0:T(8,128)(2,1)}, bf16[8,128,128]{2,1,0:T(8,128)(2,1)S(1)}, u32[]{:S(2)}, u32[]{:S(2)}) %collective-permute-start) | collective-permute-done | bytes 262176 | tf_op jit(solution)/shard_map/while/body/eval_jaxpr/ppermute | solution.py:18
  137.7 1.1 convolution_add_fusion.6
  138.8 4.3 %collective-permute-start = (bf16[8,128,128]{2,1,0:T(8,128)(2,1)}, bf16[8,128,128]{2,1,0:T(8,128)(2,1)S(1)}, u32[]{:S(2)}, u32[]{:S(2)}) collective-permute-start(bf16[8,128,128]{2,1,0:T(8,128)(2,1)} %get-tuple-element.581), channel_id=1, source_target_pairs={{0,4},{4,8},{8,12},{1,5},{5,9},{9,13},{2,6},{6,10},{10,14},{3,7},{... | collective-permute-start | bytes 786440 | tf_op jit(solution)/shard_map/while/body/eval_jaxpr/ppermute | solution.py:18
  143.1 4.2 %collective-permute-done = bf16[8,128,128]{2,1,0:T(8,128)(2,1)S(1)} collective-permute-done((bf16[8,128,128]{2,1,0:T(8,128)(2,1)}, bf16[8,128,128]{2,1,0:T(8,128)(2,1)S(1)}, u32[]{:S(2)}, u32[]{:S(2)}) %collective-permute-start) | collective-permute-done | bytes 262176 | tf_op jit(solution)/shard_map/while/body/eval_jaxpr/ppermute | solution.py:18
  148.1 1.1 convolution_add_fusion.6
  149.2 2.2 %fusion.53 = f32[2,8,128,128]{2,3,1,0:T(8,128)S(1)} fusion(f32[2,8,128,128]{2,3,1,0:T(8,128)S(1)} %copy-done.6, f32[2,8,128,128]{2,3,1,0:T(8,128)S(1)} %copy-done.3, f32[8,128,128]{2,1,0:T(8,128)} %get-tuple-element.215), kind=kOutput, calls=%fused_computation.91 | convolution fusion | flops 402915328 | bytes 3670016 | tf_op jit(solution)/shard_map/hvk,chkl->chvl/dot_general | solution.py:124
  151.4 1.1 multiply_reduce_fusion
  153.9 1.0 fusion.61
  154.9 15.6 %all_gather.6 = bf16[512,256]{1,0:T(8,128)(2,1)S(1)} all-gather(bf16[128,256]{1,0:T(8,128)(2,1)S(1)} %constant_dynamic-slice_fusion.5), channel_id=1, replica_groups=mesh['groups'=2,'seq'=4,'head'=4] {'seq'}, dimensions={0}, use_global_device_ids=true | all-gather | bytes 327680 | tf_op jit(solution)/shard_map/all_gather | solution.py:153
  170.5 14.0 %all_gather.7 = bf16[512,256]{1,0:T(8,128)(2,1)S(1)} all-gather(bf16[128,256]{1,0:T(8,128)(2,1)S(1)} %constant_dynamic-slice_fusion.4), channel_id=1, replica_groups=mesh['groups'=2,'seq'=4,'head'=4] {'seq'}, dimensions={0}, use_global_device_ids=true | all-gather | bytes 327680 | tf_op jit(solution)/shard_map/all_gather | solution.py:154
  186.1 1.2 conditional.1
  187.6 0.9 copy-done.15
  (159 shorter events, 29.1 us)
Async XLA Ops:
  0.6 154.2 %copy-start = (bf16[128,512]{1,0:T(8,128)(2,1)S(1)}, bf16[128,512]{1,0:T(8,128)(2,1)}, u32[]{:S(2)}) copy-start(bf16[128,512]{1,0:T(8,128)(2,1)} %param.27) | copy-start | bytes 393220
  2.2 0.9 copy-start.16
  3.6 1.0 copy-start.13
  5.6 0.7 copy-start.19
  6.3 0.7 copy-start.18
  53.5 1.2 copy-start.1
  53.5 1.5 copy-start.4
  55.1 2.2 %copy-start.2 = (f32[2,8,128,128]{2,3,1,0:T(8,128)}, f32[2,8,128,128]{2,3,1,0:T(8,128)S(1)}, u32[]{:S(2)}) copy-start(f32[2,8,128,128]{2,3,1,0:T(8,128)S(1)} %get-tuple-element.561) | copy-start | bytes 3145732 | tf_op jit(solution)/shard_map/while
  55.2 2.2 %copy-start.5 = (f32[2,8,128,128]{2,3,1,0:T(8,128)}, f32[2,8,128,128]{2,3,1,0:T(8,128)S(1)}, u32[]{:S(2)}) copy-start(f32[2,8,128,128]{2,3,1,0:T(8,128)S(1)} %get-tuple-element.562) | copy-start | bytes 3145732 | tf_op jit(solution)/shard_map/while
  57.3 1.0 copy-start.10
  58.4 1.0 copy-start.7
  58.8 1.0 copy-start.11
  59.8 0.8 copy-start.8
  106.3 1.2 copy-start.1
  106.3 1.5 copy-start.4
  108.0 2.2 %copy-start.2 = (f32[2,8,128,128]{2,3,1,0:T(8,128)}, f32[2,8,128,128]{2,3,1,0:T(8,128)S(1)}, u32[]{:S(2)}) copy-start(f32[2,8,128,128]{2,3,1,0:T(8,128)S(1)} %get-tuple-element.561) | copy-start | bytes 3145732 | tf_op jit(solution)/shard_map/while
  108.0 2.2 %copy-start.5 = (f32[2,8,128,128]{2,3,1,0:T(8,128)}, f32[2,8,128,128]{2,3,1,0:T(8,128)S(1)}, u32[]{:S(2)}) copy-start(f32[2,8,128,128]{2,3,1,0:T(8,128)S(1)} %get-tuple-element.562) | copy-start | bytes 3145732 | tf_op jit(solution)/shard_map/while
  110.2 1.0 copy-start.10
  111.2 1.0 copy-start.7
  111.6 1.0 copy-start.11
  112.6 0.8 copy-start.8
  114.6 34.6 %copy-start.3 = (f32[2,8,128,128]{2,3,1,0:T(8,128)S(1)}, f32[2,8,128,128]{2,3,1,0:T(8,128)}, u32[]{:S(2)}) copy-start(f32[2,8,128,128]{2,3,1,0:T(8,128)} %get-tuple-element.212) | copy-start | bytes 3145732
  114.6 34.6 %copy-start.6 = (f32[2,8,128,128]{2,3,1,0:T(8,128)S(1)}, f32[2,8,128,128]{2,3,1,0:T(8,128)}, u32[]{:S(2)}) copy-start(f32[2,8,128,128]{2,3,1,0:T(8,128)} %get-tuple-element.216) | copy-start | bytes 3145732
  114.6 11.0 %collective-permute-start = (bf16[8,128,128]{2,1,0:T(8,128)(2,1)}, bf16[8,128,128]{2,1,0:T(8,128)(2,1)S(1)}, u32[]{:S(2)}, u32[]{:S(2)}) collective-permute-start(bf16[8,128,128]{2,1,0:T(8,128)(2,1)} %get-tuple-element.581), channel_id=1, source_target_pairs={{0,4},{4,8},{8,12},{1,5},{5,9},{9,13},{2,6},{6,10},{10,14},{3,7},{... | collective-permute-start | bytes 786440 | tf_op jit(solution)/shard_map/while/body/eval_jaxpr/ppermute | solution.py:18
  127.5 9.3 %collective-permute-start = (bf16[8,128,128]{2,1,0:T(8,128)(2,1)}, bf16[8,128,128]{2,1,0:T(8,128)(2,1)S(1)}, u32[]{:S(2)}, u32[]{:S(2)}) collective-permute-start(bf16[8,128,128]{2,1,0:T(8,128)(2,1)} %get-tuple-element.581), channel_id=1, source_target_pairs={{0,4},{4,8},{8,12},{1,5},{5,9},{9,13},{2,6},{6,10},{10,14},{3,7},{... | collective-permute-start | bytes 786440 | tf_op jit(solution)/shard_map/while/body/eval_jaxpr/ppermute | solution.py:18
  138.8 8.5 %collective-permute-start = (bf16[8,128,128]{2,1,0:T(8,128)(2,1)}, bf16[8,128,128]{2,1,0:T(8,128)(2,1)S(1)}, u32[]{:S(2)}, u32[]{:S(2)}) collective-permute-start(bf16[8,128,128]{2,1,0:T(8,128)(2,1)} %get-tuple-element.581), channel_id=1, source_target_pairs={{0,4},{4,8},{8,12},{1,5},{5,9},{9,13},{2,6},{6,10},{10,14},{3,7},{... | collective-permute-start | bytes 786440 | tf_op jit(solution)/shard_map/while/body/eval_jaxpr/ppermute | solution.py:18
  149.2 2.2 %copy-start.9 = (f32[2,8,64,128]{3,2,1,0:T(8,128)S(1)}, f32[2,8,64,128]{3,2,1,0:T(8,128)}, u32[]{:S(2)}) copy-start(f32[2,8,64,128]{3,2,1,0:T(8,128)} %get-tuple-element.210) | copy-start | bytes 1572868
  149.2 2.2 %copy-start.12 = (f32[2,8,64,128]{3,2,1,0:T(8,128)S(1)}, f32[2,8,64,128]{3,2,1,0:T(8,128)}, u32[]{:S(2)}) copy-start(f32[2,8,64,128]{3,2,1,0:T(8,128)} %get-tuple-element.211) | copy-start | bytes 1572868
  152.9 1.0 copy-start.14
  154.9 15.6 %copy-start.17 = (bf16[128,512]{1,0:T(8,128)(2,1)S(1)}, bf16[128,512]{1,0:T(8,128)(2,1)}, u32[]{:S(2)}) copy-start(bf16[128,512]{1,0:T(8,128)(2,1)} %param.28) | copy-start | bytes 393220
  185.2 0.9 copy-start.22
  187.5 1.0 copy-start.15
  (2 other events, 1.3 us)
where the time goes:
time: 190 us; the launch traced here: 189 us
  other arithmetic  90.3 us (48%)
  blocking collectives  29.7 us (16%)
  matrix products  21.1 us (11%)
  local copies, waits for them, and re-layouts  17.3 us (9%)
  waiting for transfers between devices  15 us (8%)
  starting transfers between devices  13.7 us (7%)
    another operation x6, other arithmetic, block_terms(): lax.linalg.triangular_solve(system, right, left_side=True, lower=True, un...  78.8 us
    all_gather x1, blocking collectives, attend(): key_piece = lax.all_gather(keys_own, 'seq', axis=0, tiled=True)  15.6 us
    ppermute x3, waiting for transfers between devices, shifted(): return lax.ppermute(shard, axis, pairs)  15 us
    all_gather x1, blocking collectives, attend(): value_piece = lax.all_gather(values_own, 'seq', axis=0, tiled=True)  14 us
    ppermute x3, starting transfers between devices, shifted(): return lax.ppermute(shard, axis, pairs)  13.7 us
    unnamed x31, local copies, waits for them, and re-layouts  5.57 us
    while x34, local copies, waits for them, and re-layouts  4.8 us
  transfers between devices with their start and end apart: 3, of which 3 were waited for; matrix products, arithmetic and copies ran while one was open for 0% of the time, Pallas kernels for 0%

commit v1 on v0

--- a/solution.py
+++ b/solution.py
@@ -10,6 +10,20 @@
 HD_A = 256
 BLOCK = 64
 HIGH = lax.Precision.HIGHEST
+
+
+def mix_the_shelves(vals):
+    high, x_now = (jax.lax.axis_size("seq"), jax.lax.axis_index("seq"))
+    local_next, f_now = (vals, 1)
+    while f_now < high:
+        v_now = jax.lax.ppermute(
+            local_next, "seq", [(src_i, src_i ^ f_now) for src_i in range(high)]
+        )
+        odd = jnp.concatenate([local_next, v_now], 0)
+        before = jnp.concatenate([v_now, local_next], 0)
+        local_next = jnp.where(x_now & f_now == 0, odd, before)
+        f_now = 2 * f_now
+    return local_next
 
 
 def shifted(shard, axis, by):
@@ -151,7 +165,7 @@
         jnp.zeros((local_heads, length, HD_A), jnp.float32),
     )
     key_piece = lax.all_gather(keys_own, "seq", axis=0, tiled=True)
-    value_piece = lax.all_gather(values_own, "seq", axis=0, tiled=True)
+    value_piece = mix_the_shelves(values_own)
     count = key_piece.shape[0]
     width = count
     while width > 1024 and width % 2 == 0:

time: 190 us -> 182 us (0.958)
  blocking collectives: 29.7 us -> 13.8 us
  starting transfers between devices: 13.7 us -> 18.8 us
  matrix products: 21.1 us -> 24.7 us
    all_gather x1 -> x0, blocking collectives: 14 us -> none  [attend(): value_piece = lax.all_gather(values_own, 'seq', axis=0, tiled=True)]
    ppermute x0 -> x2, starting transfers between devices: none -> 7.51 us  [mix_the_shelves(): jax.lax.ppermute(local_next, 'seq', [(src_i, src_i ^ f_now) for src_i in...]
    ppermute x3, starting transfers between devices: 13.7 us -> 11.2 us  [shifted(): return lax.ppermute(shard, axis, pairs)]
    dot_general x3, matrix products: 3.32 us -> 1.2 us  [relay(): jnp.einsum('hvk,hkl->hvl', incoming, device_map, precision=HIGH)]
    unnamed x31 -> x29, local copies, waits for them, and re-layouts: 5.57 us -> 7 us
    while x34 -> x50, local copies, waits for them, and re-layouts: 4.8 us -> 3.54 us
  transfers between devices with their start and end apart: 3 -> 5, of which waited for: 3 -> 3; matrix products, arithmetic and copies ran while one was open for 0% -> 65% of each run, Pallas kernels for 0% -> 0%
where the time goes in v1:
time: 182 us; the launch traced here: 181 us
  other arithmetic  91.5 us (50%)
  matrix products  24.7 us (14%)
  starting transfers between devices  18.8 us (10%)
  local copies, waits for them, and re-layouts  16.5 us (9%)
  waiting for transfers between devices  13.8 us (8%)
  blocking collectives  13.8 us (8%)
    another operation x6, other arithmetic, block_terms(): lax.linalg.triangular_solve(system, right, left_side=True, lower=True, un...  80.3 us
    all_gather x1, blocking collectives, attend(): key_piece = lax.all_gather(keys_own, 'seq', axis=0, tiled=True)  13.8 us
    ppermute x3, waiting for transfers between devices, shifted(): return lax.ppermute(shard, axis, pairs)  13.8 us
    ppermute x3, starting transfers between devices, shifted(): return lax.ppermute(shard, axis, pairs)  11.2 us
    ppermute x2, starting transfers between devices, mix_the_shelves(): jax.lax.ppermute(local_next, 'seq', [(src_i, src_i ^ f_now) for src_i in...  7.51 us
    unnamed x29, local copies, waits for them, and re-layouts  7 us
  transfers between devices with their start and end apart: 5, of which 3 were waited for; matrix products, arithmetic and copies ran while one was open for 65% of the time, Pallas kernels for 0%

profile of v1, /device:TPU:0, one launch (start us, length us, event | category | flops | bytes accessed | tf_op | source)
XLA Modules:
  0.0 181.5 jit_solution(8703834445420237085)
XLA Ops:
  2.2 3.1 %collective-permute-start.1 = (bf16[128,256]{1,0:T(8,128)(2,1)}, bf16[128,256]{1,0:T(8,128)(2,1)}, u32[]{:S(2)}, u32[]{:S(2)}) collective-permute-start(bf16[128,256]{1,0:T(8,128)(2,1)} %constant_dynamic-slice_fusion.4), channel_id=1, source_target_pairs={{0,4},{4,0},{8,12},{12,8},{1,5},{5,1},{9,13},{13,9},{2,6},{6,2},{1... | collective-permute-start | bytes 196616 | tf_op jit(solution)/shard_map/ppermute | solution.py:19
  5.9 1.2 fusion.66
  12.5 109.1 %while.13 = (s32[]{:T(128)}, f32[8,128,128]{1,2,0:T(8,128)S(1)}, f32[8,128,128]{1,2,0:T(8,128)S(1)}, f32[2,8,64,128]{3,2,1,0:T(8,128)}, f32[2,8,64,128]{3,2,1,0:...) while((s32[]{:T(128)}, f32[8,128,128]{1,2,0:T(8,128)S(1)}, ...), condition=%wide.region_4.5_spmd.clone, body=%wide.region_2.4_spmd.clone.sunk | while | flops 907780864 | bytes 36036276 | solution.py:134
  15.4 1.3 fusion.126
  16.7 40.0 %custom-call.11 = f32[8,1,64,64]{2,3,1,0:T(8,128)S(1)} custom-call(f32[8,1,64,64]{3,2,1,0:T(8,128)} %fusion.126), custom_call_target="InvertDiagBlocksLowerTriangular" | custom-call | tf_op jit(solution)/shard_map/while/body/eval_jaxpr/triangular_solve | solution.py:59
  58.7 1.1 convolution_subtract_fusion.3
  59.8 1.0 convolution_bitcast_fusion.7
  61.5 1.1 convolution_add_fusion.7
  62.6 1.0 convolution_bitcast_fusion.6
  64.2 1.1 fusion.129
  65.3 1.1 fusion.128
  69.9 1.3 fusion.126
  71.2 40.0 %custom-call.11 = f32[8,1,64,64]{2,3,1,0:T(8,128)S(1)} custom-call(f32[8,1,64,64]{3,2,1,0:T(8,128)} %fusion.126), custom_call_target="InvertDiagBlocksLowerTriangular" | custom-call | tf_op jit(solution)/shard_map/while/body/eval_jaxpr/triangular_solve | solution.py:59
  113.3 1.1 convolution_subtract_fusion.3
  114.4 1.0 convolution_bitcast_fusion.7
  116.0 1.1 convolution_add_fusion.7
  117.1 1.0 convolution_bitcast_fusion.6
  118.7 1.1 fusion.129
  119.8 1.1 fusion.128
  122.1 28.8 %while.12 = (s32[]{:T(128)}, f32[8,128,128]{2,1,0:T(8,128)}, bf16[8,128,128]{2,1,0:T(8,128)(2,1)S(1)}, f32[8,128,128]{2,1,0:T(8,128)S(1)}, f32[8,128,128]{2,1,0:T(8,128)S(1)}, /*index=5*/s32[]{:T(128)}) while((s32[]{:T(128)}, f32[8,128,128]{2,1,0:T(8,128)}, bf16[8,128,128]{2,1,0:T(8,128)(2,1)S(1)}, f32[8,128,128]{2,1,0:T(8,128)S(1)}, ...), condition=%wide.region_6.7_spmd, body=%wide.region_5.6_spmd.sunk | while | flops 201719808 | bytes 3407981 | solution.py:90
  122.1 2.1 %collective-permute-start = (bf16[8,128,128]{2,1,0:T(8,128)(2,1)S(1)}, bf16[8,128,128]{2,1,0:T(8,128)(2,1)S(1)}, u32[]{:S(2)}, u32[]{:S(2)}) collective-permute-start(bf16[8,128,128]{2,1,0:T(8,128)(2,1)S(1)} %get-tuple-element.606), channel_id=1, source_target_pairs={{0,4},{4,8},{8,12},{1,5},{5,9},{9,13},{2,6},{6,10},{10,14},{3,7},{... | collective-permute-start | bytes 786440 | tf_op jit(solution)/shard_map/while/body/eval_jaxpr/ppermute | solution.py:32
  124.2 5.5 %collective-permute-done = bf16[8,128,128]{2,1,0:T(8,128)(2,1)S(1)} collective-permute-done((bf16[8,128,128]{2,1,0:T(8,128)(2,1)S(1)}, bf16[8,128,128]{2,1,0:T(8,128)(2,1)S(1)}, u32[]{:S(2)}, u32[]{:S(2)}) %collective-permute-start) | collective-permute-done | bytes 262176 | tf_op jit(solution)/shard_map/while/body/eval_jaxpr/ppermute | solution.py:32
  130.9 4.8 %collective-permute-start = (bf16[8,128,128]{2,1,0:T(8,128)(2,1)S(1)}, bf16[8,128,128]{2,1,0:T(8,128)(2,1)S(1)}, u32[]{:S(2)}, u32[]{:S(2)}) collective-permute-start(bf16[8,128,128]{2,1,0:T(8,128)(2,1)S(1)} %get-tuple-element.606), channel_id=1, source_target_pairs={{0,4},{4,8},{8,12},{1,5},{5,9},{9,13},{2,6},{6,10},{10,14},{3,7},{... | collective-permute-start | bytes 786440 | tf_op jit(solution)/shard_map/while/body/eval_jaxpr/ppermute | solution.py:32
  135.8 4.4 %collective-permute-done = bf16[8,128,128]{2,1,0:T(8,128)(2,1)S(1)} collective-permute-done((bf16[8,128,128]{2,1,0:T(8,128)(2,1)S(1)}, bf16[8,128,128]{2,1,0:T(8,128)(2,1)S(1)}, u32[]{:S(2)}, u32[]{:S(2)}) %collective-permute-start) | collective-permute-done | bytes 262176 | tf_op jit(solution)/shard_map/while/body/eval_jaxpr/ppermute | solution.py:32
  141.4 4.4 %collective-permute-start = (bf16[8,128,128]{2,1,0:T(8,128)(2,1)S(1)}, bf16[8,128,128]{2,1,0:T(8,128)(2,1)S(1)}, u32[]{:S(2)}, u32[]{:S(2)}) collective-permute-start(bf16[8,128,128]{2,1,0:T(8,128)(2,1)S(1)} %get-tuple-element.606), channel_id=1, source_target_pairs={{0,4},{4,8},{8,12},{1,5},{5,9},{9,13},{2,6},{6,10},{10,14},{3,7},{... | collective-permute-start | bytes 786440 | tf_op jit(solution)/shard_map/while/body/eval_jaxpr/ppermute | solution.py:32
  145.8 3.9 %collective-permute-done = bf16[8,128,128]{2,1,0:T(8,128)(2,1)S(1)} collective-permute-done((bf16[8,128,128]{2,1,0:T(8,128)(2,1)S(1)}, bf16[8,128,128]{2,1,0:T(8,128)(2,1)S(1)}, u32[]{:S(2)}, u32[]{:S(2)}) %collective-permute-start) | collective-permute-done | bytes 262176 | tf_op jit(solution)/shard_map/while/body/eval_jaxpr/ppermute | solution.py:32
  150.9 2.4 %fusion.55 = f32[2,8,128,128]{2,3,1,0:T(8,128)S(1)} fusion(f32[2,8,128,128]{2,3,1,0:T(8,128)} %get-tuple-element.234, f32[2,8,128,128]{2,3,1,0:T(8,128)S(1)} %copy-done.5, f32[8,128,128]{2,1,0:T(8,128)} %get-tuple-element.233), kind=kOutput, calls=%fused_computation.93 | convolution fusion | flops 402915328 | bytes 3670016 | tf_op jit(solution)/shard_map/hvk,chkl->chvl/dot_general | solution.py:138
  153.4 2.4 %multiply_reduce_fusion = (f32[2,64,8]{1,2,0:T(8,128)S(1)}, f32[2,64,8,128]{3,1,2,0:T(8,128)S(1)}) fusion(f32[2,8,64,128]{3,2,1,0:T(8,128)} %get-tuple-element.228, f32[2,8,64,128]{3,2,1,0:T(8,128)} %get-tuple-element.229, f32[2,8,128,128]{2,3,1,0:T(8,128)S(1)} %fusion.55), kind=kOutput, calls=%fused_computation.109 | convolution fusion | flops 201718784 | bytes 2625536 | tf_op jit(solution)/shard_map/chik,chvk->chiv/dot_general | solution.py:139
  157.4 4.5 %collective-permute-start.2 = (bf16[256,256]{1,0:T(8,128)(2,1)S(1)}, bf16[256,256]{1,0:T(8,128)(2,1)S(1)}, u32[]{:S(2)}, u32[]{:S(2)}) collective-permute-start(bf16[256,256]{1,0:T(8,128)(2,1)S(1)} %maximum_select_fusion), channel_id=1, source_target_pairs={{0,8},{4,12},{8,0},{12,4},{1,9},{5,13},{9,1},{13,5},{2,10},{6,14},... | collective-permute-start | bytes 393224 | tf_op jit(solution)/shard_map/ppermute | solution.py:19
  161.9 13.8 %all_gather.3 = bf16[512,256]{1,0:T(8,128)(2,1)S(1)} all-gather(bf16[128,256]{1,0:T(8,128)(2,1)S(1)} %constant_dynamic-slice_fusion.5), channel_id=1, replica_groups=mesh['groups'=2,'seq'=4,'head'=4] {'seq'}, dimensions={0}, use_global_device_ids=true | all-gather | bytes 327680 | tf_op jit(solution)/shard_map/all_gather | solution.py:167
  177.8 1.2 conditional.1
  180.3 1.2 multiply_convert_fusion
  (178 shorter events, 30.0 us)
Async XLA Ops:
  0.6 0.9 copy-start
  0.7 6.6 %copy-start.11 = (bf16[128,512]{1,0:T(8,128)(2,1)S(1)}, bf16[128,512]{1,0:T(8,128)(2,1)}, u32[]{:S(2)}) copy-start(bf16[128,512]{1,0:T(8,128)(2,1)} %param.20) | copy-start | bytes 393220
  2.2 154.3 %collective-permute-start.1 = (bf16[128,256]{1,0:T(8,128)(2,1)}, bf16[128,256]{1,0:T(8,128)(2,1)}, u32[]{:S(2)}, u32[]{:S(2)}) collective-permute-start(bf16[128,256]{1,0:T(8,128)(2,1)} %constant_dynamic-slice_fusion.4), channel_id=1, source_target_pairs={{0,4},{4,0},{8,12},{12,8},{1,5},{5,1},{9,13},{13,9},{2,6},{6,2},{1... | collective-permute-start | bytes 196616 | tf_op jit(solution)/shard_map/ppermute | solution.py:19
  7.8 0.9 copy-start.12
  9.2 1.0 copy-start.8
  12.5 1.8 %copy-start.13 = (f32[2,8,64]{2,0,1:T(2,128)}, f32[2,8,64]{2,0,1:T(2,128)S(1)}, u32[]{:S(2)}) copy-start(f32[2,8,64]{2,0,1:T(2,128)S(1)} %get-tuple-element.591) | copy-start | bytes 12292 | tf_op jit(solution)/shard_map/while
  12.5 44.2 %copy-start.16 = (s32[2,64]{1,0:T(2,128)}, s32[2,64]{1,0:T(2,128)S(1)}, u32[]{:S(2)}) copy-start(s32[2,64]{1,0:T(2,128)S(1)} %get-tuple-element.589) | copy-start | bytes 1540 | tf_op jit(solution)/shard_map/while
  12.5 44.9 %copy-start.1 = (f32[2,8,64,128]{3,1,2,0:T(8,128)}, f32[2,8,64,128]{3,1,2,0:T(8,128)S(1)}, u32[]{:S(2)}) copy-start(f32[2,8,64,128]{3,1,2,0:T(8,128)S(1)} %get-tuple-element.593) | copy-start | bytes 1572868 | tf_op jit(solution)/shard_map/while
  59.8 1.2 copy-start.3
  59.8 1.5 copy-start.6
  61.4 2.1 %copy-start.4 = (f32[2,8,128,128]{2,3,1,0:T(8,128)}, f32[2,8,128,128]{2,3,1,0:T(8,128)S(1)}, u32[]{:S(2)}) copy-start(f32[2,8,128,128]{2,3,1,0:T(8,128)S(1)} %get-tuple-element.586) | copy-start | bytes 3145732 | tf_op jit(solution)/shard_map/while
  61.5 2.1 %copy-start.7 = (f32[2,8,128,128]{2,3,1,0:T(8,128)}, f32[2,8,128,128]{2,3,1,0:T(8,128)S(1)}, u32[]{:S(2)}) copy-start(f32[2,8,128,128]{2,3,1,0:T(8,128)S(1)} %get-tuple-element.587) | copy-start | bytes 3145732 | tf_op jit(solution)/shard_map/while
  65.3 1.1 copy-start.2
  66.4 0.7 copy-start.25
  67.1 1.8 %copy-start.13 = (f32[2,8,64]{2,0,1:T(2,128)}, f32[2,8,64]{2,0,1:T(2,128)S(1)}, u32[]{:S(2)}) copy-start(f32[2,8,64]{2,0,1:T(2,128)S(1)} %get-tuple-element.591) | copy-start | bytes 12292 | tf_op jit(solution)/shard_map/while
  67.1 44.2 %copy-start.16 = (s32[2,64]{1,0:T(2,128)}, s32[2,64]{1,0:T(2,128)S(1)}, u32[]{:S(2)}) copy-start(s32[2,64]{1,0:T(2,128)S(1)} %get-tuple-element.589) | copy-start | bytes 1540 | tf_op jit(solution)/shard_map/while
  67.1 44.9 %copy-start.1 = (f32[2,8,64,128]{3,1,2,0:T(8,128)}, f32[2,8,64,128]{3,1,2,0:T(8,128)S(1)}, u32[]{:S(2)}) copy-start(f32[2,8,64,128]{3,1,2,0:T(8,128)S(1)} %get-tuple-element.593) | copy-start | bytes 1572868 | tf_op jit(solution)/shard_map/while
  114.4 1.2 copy-start.3
  114.4 1.5 copy-start.6
  116.0 2.1 %copy-start.4 = (f32[2,8,128,128]{2,3,1,0:T(8,128)}, f32[2,8,128,128]{2,3,1,0:T(8,128)S(1)}, u32[]{:S(2)}) copy-start(f32[2,8,128,128]{2,3,1,0:T(8,128)S(1)} %get-tuple-element.586) | copy-start | bytes 3145732 | tf_op jit(solution)/shard_map/while
  116.0 2.1 %copy-start.7 = (f32[2,8,128,128]{2,3,1,0:T(8,128)}, f32[2,8,128,128]{2,3,1,0:T(8,128)S(1)}, u32[]{:S(2)}) copy-start(f32[2,8,128,128]{2,3,1,0:T(8,128)S(1)} %get-tuple-element.587) | copy-start | bytes 3145732 | tf_op jit(solution)/shard_map/while
  119.8 1.1 copy-start.2
  122.1 28.8 %copy-start.5 = (f32[2,8,128,128]{2,3,1,0:T(8,128)S(1)}, f32[2,8,128,128]{2,3,1,0:T(8,128)}, u32[]{:S(2)}) copy-start(f32[2,8,128,128]{2,3,1,0:T(8,128)} %get-tuple-element.230) | copy-start | bytes 3145732
  122.1 7.6 %collective-permute-start = (bf16[8,128,128]{2,1,0:T(8,128)(2,1)S(1)}, bf16[8,128,128]{2,1,0:T(8,128)(2,1)S(1)}, u32[]{:S(2)}, u32[]{:S(2)}) collective-permute-start(bf16[8,128,128]{2,1,0:T(8,128)(2,1)S(1)} %get-tuple-element.606), channel_id=1, source_target_pairs={{0,4},{4,8},{8,12},{1,5},{5,9},{9,13},{2,6},{6,10},{10,14},{3,7},{... | collective-permute-start | bytes 786440 | tf_op jit(solution)/shard_map/while/body/eval_jaxpr/ppermute | solution.py:32
  130.9 9.2 %collective-permute-start = (bf16[8,128,128]{2,1,0:T(8,128)(2,1)S(1)}, bf16[8,128,128]{2,1,0:T(8,128)(2,1)S(1)}, u32[]{:S(2)}, u32[]{:S(2)}) collective-permute-start(bf16[8,128,128]{2,1,0:T(8,128)(2,1)S(1)} %get-tuple-element.606), channel_id=1, source_target_pairs={{0,4},{4,8},{8,12},{1,5},{5,9},{9,13},{2,6},{6,10},{10,14},{3,7},{... | collective-permute-start | bytes 786440 | tf_op jit(solution)/shard_map/while/body/eval_jaxpr/ppermute | solution.py:32
  141.4 8.3 %collective-permute-start = (bf16[8,128,128]{2,1,0:T(8,128)(2,1)S(1)}, bf16[8,128,128]{2,1,0:T(8,128)(2,1)S(1)}, u32[]{:S(2)}, u32[]{:S(2)}) collective-permute-start(bf16[8,128,128]{2,1,0:T(8,128)(2,1)S(1)} %get-tuple-element.606), channel_id=1, source_target_pairs={{0,4},{4,8},{8,12},{1,5},{5,9},{9,13},{2,6},{6,10},{10,14},{3,7},{... | collective-permute-start | bytes 786440 | tf_op jit(solution)/shard_map/while/body/eval_jaxpr/ppermute | solution.py:32
  153.4 3.1 %copy-start.15 = (bf16[128,512]{1,0:T(8,128)(2,1)S(1)}, bf16[128,512]{1,0:T(8,128)(2,1)}, u32[]{:S(2)}) copy-start(bf16[128,512]{1,0:T(8,128)(2,1)} %param.27) | copy-start | bytes 393220
  157.4 19.5 %collective-permute-start.2 = (bf16[256,256]{1,0:T(8,128)(2,1)S(1)}, bf16[256,256]{1,0:T(8,128)(2,1)S(1)}, u32[]{:S(2)}, u32[]{:S(2)}) collective-permute-start(bf16[256,256]{1,0:T(8,128)(2,1)S(1)} %maximum_select_fusion), channel_id=1, source_target_pairs={{0,8},{4,12},{8,0},{12,4},{1,9},{5,13},{9,1},{13,5},{2,10},{6,14},... | collective-permute-start | bytes 393224 | tf_op jit(solution)/shard_map/ppermute | solution.py:19
  176.9 1.0 copy-start.23
  176.9 0.9 copy-start.20
  179.3 1.0 copy-start.9
  179.3 1.0 copy-start.10
  (11 other events, 7.3 us)
